TPU v7x, 32 devices: a whole 2x2x4 slice. The times are simulated.
32 devices in a mesh: groups: 2 (over y), ep: 4 (over z), half: 2 (over x), tp: 2 (over core).
Axes of the slice: x: 2, y: 2, z: 4, core: 2. Of those that a mesh axis runs over, the one named last changes fastest.
Arguments:
- queries: bfloat16 [512, 2048], P(('groups', 'ep', 'half'), 'tp'), parts along dimension 0, may hold values from -6 to 6
- new_keys: bfloat16 [512, 256], P(('groups', 'ep', 'half'), 'tp'), parts along dimension 0, may hold values from -4 to 4
- new_values: bfloat16 [512, 256], P(('groups', 'ep', 'half'), 'tp'), parts along dimension 0, may hold values from -4 to 4
- cache_keys: bfloat16 [512, 2, 64, 128], P(('groups', 'ep', 'half'), 'tp'), parts along dimension 0, may hold values from -4 to 4
- cache_values: bfloat16 [512, 2, 64, 128], P(('groups', 'ep', 'half'), 'tp'), parts along dimension 0, may hold values from -4 to 4
- lengths: int32 [512], P(('groups', 'ep', 'half')), parts along dimension 0, may hold values from 1 to 64, as said below
- out_weight: bfloat16 [2048, 2048], P('tp', 'half'), may hold values from -0.375 to 0.375
- residual: bfloat16 [512, 2048], P(('groups', 'ep'), 'half'), parts along dimension 0, may hold values from -5 to 5
- norm_gain: float32 [2048], P('half'), may hold values from 0.1 to 1.9
- expert_ids: int32 [512, 8], P(('groups', 'ep')), parts along dimension 0, may hold values from 0 to 63, all different within a row; in each aligned block of 64 rows (0 to 63, 64 to 127, ...) at most 12 rows name the same one
- gate_weights: float32 [512, 8], P(('groups', 'ep')), parts along dimension 0, may hold values from 0.05 to 1
- w_gate: bfloat16 [64, 768, 2048], P(('ep', 'tp'), 'half'), may hold values from -0.125 to 0.125
- w_up: bfloat16 [64, 768, 2048], P(('ep', 'tp'), 'half'), may hold values from -0.125 to 0.125
- w_down: bfloat16 [64, 768, 2048], P(('ep', 'tp'), 'half'), may hold values from -0.625 to 0.625
Outputs:
- layer_out: bfloat16 [512, 2048], P(('groups', 'ep'), ('half', 'tp')), parts along dimension 0
There are 2 independent parts, one for each index of `groups`. A program takes and returns all parts, laid end to end along the dimension named above; an argument that names none is the same for every part. Nothing has to cross between parts.
Inputs may be any that keep to these rules, and one draw needn't show every extreme that they name: `expert_ids`: in each block of 64 consecutive rows (the tokens of one index of ep) no expert is named by more than 12 rows. `lengths`: among each device's 32 requests one has 64 cached tokens.
All inputs are finite; a program needn't handle non-finite values.
Results may differ from a plain program's by a relative error of at most 0.014.
Values may be sent and summed in bfloat16 or wider, within the bound.
No kernel may reach another device: no remote copies, remote signals or barrier semaphores. Data moves between devices by JAX's collectives and lax.ppermute only.
A program may use at most 128 MiB of HBM per device.

v0:
```python
import math
import jax
import jax.numpy as jnp
from jax import lax
from jax.sharding import PartitionSpec as P

EXPERTS = 64
EPSILON = 1e-06


def attend(queries, new_keys, new_values, cache_keys, cache_values, lengths):
    requests, key_heads, context, head_size = cache_keys.shape
    sharing = queries.shape[1] // (key_heads * head_size)
    query_blocks = queries.reshape(requests, key_heads, sharing, head_size)
    score_scale = 1.0 / math.sqrt(head_size)
    scores = (
        jnp.einsum("rkgd,rkcd->rkgc", query_blocks, cache_keys, preferred_element_type=jnp.float32)
        * score_scale
    )
    own_score = (
        jnp.einsum(
            "rkgd,rkd->rkg",
            query_blocks,
            new_keys.reshape(requests, key_heads, head_size),
            preferred_element_type=jnp.float32,
        )
        * score_scale
    )
    valid = lax.iota(jnp.int32, context)[None, :] < lengths[:, None]
    scores = jnp.where(valid[:, None, None, :], scores, -1e30)
    highest = jnp.maximum(jnp.max(scores, axis=-1), own_score)
    weights = jnp.exp(scores - highest[..., None])
    own_weight = jnp.exp(own_score - highest)
    denominator = jnp.sum(weights, axis=-1) + own_weight
    probs = (weights / denominator[..., None]).astype(jnp.bfloat16)
    own_prob = (own_weight / denominator).astype(jnp.bfloat16)
    mixture = jnp.einsum("rkgc,rkcd->rkgd", probs, cache_values, preferred_element_type=jnp.float32)
    mixture = mixture + own_prob.astype(jnp.float32)[..., None] * new_values.reshape(
        requests, key_heads, 1, head_size
    ).astype(jnp.float32)
    return mixture.astype(jnp.bfloat16).reshape(requests, key_heads * sharing * head_size)


def combine_rows(returned_rows, target, gates):
    token_rows, top_count = target.shape
    safe_target = jnp.maximum(target, 0).reshape(-1)
    picked = jnp.take(returned_rows, safe_target, axis=0).reshape(
        token_rows, top_count, returned_rows.shape[1]
    )
    weighting = jnp.where(target >= 0, gates, 0.0)
    return jnp.sum(picked.astype(jnp.float32) * weighting[..., None], axis=1)


def on_device(
    queries,
    new_keys,
    new_values,
    cache_keys,
    cache_values,
    lengths,
    out_weight,
    residual,
    norm_gain,
    expert_ids,
    gate_weights,
    w_gate,
    w_up,
    w_down,
):
    attended = attend(queries, new_keys, new_values, cache_keys, cache_values, lengths)
    partial_mix = jnp.dot(
        lax.all_gather(attended, "half", axis=0, tiled=True),
        out_weight,
        preferred_element_type=jnp.float32,
    )
    mixed = lax.psum(partial_mix.astype(jnp.bfloat16), "tp").astype(jnp.float32)
    hidden = residual.astype(jnp.float32) + mixed
    squares = lax.psum(jnp.sum(hidden * hidden, axis=1), "half")
    half_width = hidden.shape[1]
    width = half_width * lax.axis_size("half")
    normed = (hidden * lax.rsqrt(squares / width + EPSILON)[:, None] * norm_gain[None, :]).astype(
        jnp.bfloat16
    )
    token_rows, top_count = expert_ids.shape
    ep_count = lax.axis_size("ep")
    tp_count = lax.axis_size("tp")
    local_experts = w_gate.shape[0]
    capacity = token_rows * top_count * 3 // (2 * EXPERTS)
    slot_count = ep_count * local_experts * capacity
    flat_ids = expert_ids.reshape(-1)
    one_hot = (flat_ids[:, None] == lax.iota(jnp.int32, EXPERTS)[None, :]).astype(jnp.int32)
    earlier = jnp.cumsum(one_hot, axis=0) - one_hot
    slot = jnp.sum(earlier * one_hot, axis=1)
    owner_ep = flat_ids // (local_experts * tp_count)
    owner_tp = flat_ids // local_experts % tp_count
    target = owner_ep * (local_experts * capacity) + flat_ids % local_experts * capacity + slot
    target = jnp.where(owner_tp == lax.axis_index("tp"), target, -1).reshape(token_rows, top_count)
    dispatch_matrix = jnp.any(
        lax.iota(jnp.int32, slot_count)[:, None, None] == target[None, :, :], axis=2
    ).astype(jnp.bfloat16)
    gates = gate_weights / jnp.sum(gate_weights, axis=1, keepdims=True)
    full_rows = lax.all_gather(normed, "half", axis=1, tiled=True)
    outgoing = jnp.dot(dispatch_matrix, full_rows, preferred_element_type=jnp.float32).astype(
        jnp.bfloat16
    )
    arrived = lax.all_to_all(
        outgoing.reshape(ep_count, local_experts, capacity, width),
        "ep",
        split_axis=0,
        concat_axis=0,
        tiled=True,
    )
    gate_part = jnp.einsum("secd,efd->secf", arrived, w_gate, preferred_element_type=jnp.float32)
    up_part = jnp.einsum("secd,efd->secf", arrived, w_up, preferred_element_type=jnp.float32)
    activation = (jax.nn.silu(gate_part) * up_part).astype(jnp.bfloat16)
    expert_out = jnp.einsum(
        "secf,efd->secd", activation, w_down, preferred_element_type=jnp.float32
    ).astype(jnp.bfloat16)
    summed = lax.psum_scatter(
        expert_out.astype(jnp.float32).astype(jnp.bfloat16), "half", scatter_dimension=3, tiled=True
    ).astype(jnp.float32)
    returned = lax.all_to_all(
        summed.reshape(ep_count, local_experts * capacity, half_width).astype(jnp.bfloat16),
        "ep",
        split_axis=0,
        concat_axis=0,
        tiled=True,
    ).astype(jnp.float32)
    term = combine_rows(returned.reshape(slot_count, half_width), target, gates)
    expert_sum = lax.psum_scatter(
        term.astype(jnp.bfloat16), "tp", scatter_dimension=1, tiled=True
    ).astype(jnp.float32)
    slice_width = expert_sum.shape[1]
    own_columns = lax.dynamic_slice_in_dim(
        hidden, lax.axis_index("tp") * slice_width, slice_width, 1
    )
    return (own_columns + expert_sum).astype(jnp.bfloat16)


def solution(mesh):
    placed = (
        P(("groups", "ep", "half"), "tp"),
        P(("groups", "ep", "half"), "tp"),
        P(("groups", "ep", "half"), "tp"),
        P(("groups", "ep", "half"), "tp", None, None),
        P(("groups", "ep", "half"), "tp", None, None),
        P(("groups", "ep", "half")),
        P("tp", "half"),
        P(("groups", "ep"), "half"),
        P("half"),
        P(("groups", "ep"), None),
        P(("groups", "ep"), None),
        P(("ep", "tp"), "half", None),
        P(("ep", "tp"), "half", None),
        P(("ep", "tp"), "half", None),
    )
    return jax.shard_map(
        on_device,
        mesh=mesh,
        in_specs=placed,
        out_specs=P(("groups", "ep"), ("half", "tp")),
        check_vma=False,
    )
```

profile of v0, /device:TPU:0, one launch (start us, length us, event | category | flops | bytes accessed | tf_op | source)
XLA Modules:
  0.0 210.5 jit_solution(17106588360139845303)
XLA Ops:
  6.5 1.0 copy.78
  7.5 0.7 iota_compare_fusion.3
  8.3 0.8 fusion.58
  9.1 1.5 fusion.76
  10.6 0.2 fusion.55
  10.9 0.7 convert_element_type.73
  11.6 1.4 fusion.41
  13.0 6.0 %all_gather.6 = bf16[64,1024]{1,0:T(8,128)(2,1)S(1)} all-gather(bf16[32,1024]{1,0:T(8,128)(2,1)S(1)} %bitcast.97), channel_id=1, replica_groups=mesh['groups'=2,'ep'=4,'half'=2,'tp'=2] {'half'}, dimensions={0}, use_global_device_ids=true | all-gather | bytes 196608 | tf_op jit(solution)/shard_map/all_gather | solution.py:72
  19.0 1.1 convolution_convert_fusion.1
  20.1 0.0 reduce-scatter.3.cloned.1.call-start
  20.2 0.1 copy.59
  20.3 0.1 eq.56
  20.4 0.1 eq.52
  20.5 1.2 reduce-window.6
  21.7 0.2 slice_reduce_fusion
  22.0 0.1 fusion.53
  22.1 0.1 reduce_sum.49
  22.2 0.1 copy.62
  22.3 0.1 copy.64
  22.4 0.3 fusion.47
  22.7 17.3 %all-reduce.2.cloned.1.call-done = bf16[64,1024]{1,0:T(8,128)(2,1)} async-done(((bf16[64,1024]{1,0:T(8,128)(2,1)}), bf16[64,1024]{1,0:T(8,128)(2,1)}) %all-reduce.2.cloned.1.call-update) | async-done | bytes 131088 | tf_op jit(solution)/shard_map/psum | solution.py:76
  40.0 1.0 convert_add_fusion
  41.0 4.9 %psum.15 = f32[64]{0:T(128)S(1)} all-reduce(f32[64]{0:T(128)S(1)} %get-tuple-element.8), channel_id=1, replica_groups=mesh['groups'=2,'ep'=4,'half'=2,'tp'=2] {'half'}, use_global_device_ids=true, to_apply=%region_8.9 | all-reduce | flops 64 | bytes 512 | tf_op jit(solution)/shard_map/psum | solution.py:78
  46.0 1.0 multiply_convert_fusion
  47.0 5.6 %all_gather.7 = bf16[64,2048]{1,0:T(8,128)(2,1)S(1)} all-gather(bf16[64,1024]{1,0:T(8,128)(2,1)S(1)} %multiply_convert_fusion), channel_id=1, replica_groups=mesh['groups'=2,'ep'=4,'half'=2,'tp'=2] {'half'}, dimensions={1}, use_global_device_ids=true | all-gather | bytes 393216 | tf_op jit(solution)/shard_map/all_gather | solution.py:102
  52.6 1.8 convolution_convert_fusion
  54.4 3.6 %reshape.224 = bf16[4,8,12,2048]{3,2,1,0:T(8,128)(2,1)} reshape(bf16[384,2048]{1,0:T(8,128)(2,1)} %convolution_convert_fusion) | data formatting | bytes 3145728 | tf_op jit(solution)/shard_map/reshape | solution.py:107
  58.0 2.5 %copy.65 = bf16[4,8,12,2048]{3,1,2,0:T(8,128)(2,1)S(1)} copy(bf16[4,8,12,2048]{3,2,1,0:T(8,128)(2,1)} %reshape.224) | data formatting | bytes 3145728 | tf_op jit(solution)/shard_map/reshape | solution.py:107
  60.5 39.8 %all_to_all.10 = bf16[4,8,12,2048]{3,1,2,0:T(8,128)(2,1)S(1)} all-to-all(bf16[4,8,12,2048]{3,1,2,0:T(8,128)(2,1)S(1)} %copy.65), channel_id=1, replica_groups=mesh['groups'=2,'ep'=4,'half'=2,'tp'=2] {'ep'}, dimensions={0} | all-to-all | bytes 3145728 | tf_op jit(solution)/shard_map/all_to_all | solution.py:106
  100.2 1.1 copy-done.1
  101.4 8.7 %fusion.16 = f32[4,8,12,384]{3,2,0,1:T(8,128)S(1)} fusion(bf16[8,384,2048]{2,1,0:T(8,128)(2,1)} %param.25, bf16[4,8,12,2048]{3,1,2,0:T(8,128)(2,1)S(1)} %all_to_all.10), kind=kOutput, calls=%fused_computation.15 | convolution fusion | flops 603979776 | bytes 14745600 | tf_op jit(solution)/shard_map/secd,efd->secf/dot_general | solution.py:113
  110.1 18.4 %fusion.9 = bf16[4,8,12,2048]{3,2,0,1:T(8,128)(2,1)} fusion(bf16[8,384,2048]{2,1,0:T(8,128)(2,1)} %param.27, bf16[8,384,2048]{2,1,0:T(8,128)(2,1)} %param.26, bf16[4,8,12,2048]{3,1,2,0:T(8,128)(2,1)} %copy-done.1, f32[4,8,12,384]{3,2,0,1:T(8,128)S(1)} %fusion.16), kind=kOutput, calls=%fused_computation.9 | convolution fusion | flops 1209630720 | bytes 28901376 | tf_op jit(solution)/shard_map/secf,efd->secd/dot_general | solution.py:116
  128.5 0.0 reduce-scatter.3.cloned.1.call-update
  128.5 31.1 %reduce-scatter.3.cloned.1.call-done = bf16[4,8,12,1024]{3,2,0,1:T(8,128)(2,1)} async-done(((bf16[4,8,12,2048]{3,2,0,1:T(8,128)(2,1)}), bf16[4,8,12,1024]{3,2,0,1:T(8,128)(2,1)}) %reduce-scatter.3.cloned.1.call-update) | async-done | bytes 786448 | tf_op jit(solution)/shard_map/reduce_scatter | solution.py:119
  159.6 1.8 copy.68
  161.4 1.1 copy.69
  162.5 4.6 %all-to-all-start.1 = ((bf16[4,96,1024]{2,1,0:T(8,128)(2,1)}), bf16[4,96,1024]{2,1,0:T(8,128)(2,1)S(1)}, u32[]{:S(2)}, u32[]{:S(2)}) async-start(bf16[4,96,1024]{2,1,0:T(8,128)(2,1)} %copy.69), calls=%async_computation.2 | async-start | bytes 1572864 | tf_op jit(solution)/shard_map/all_to_all | solution.py:122
  167.1 0.1 copy.70
  167.2 0.1 reshape.227
  167.3 0.1 copy.71
  167.4 0.1 copy.63
  167.6 19.5 %all-to-all-done.1 = bf16[4,96,1024]{2,1,0:T(8,128)(2,1)S(1)} async-done(((bf16[4,96,1024]{2,1,0:T(8,128)(2,1)}), bf16[4,96,1024]{2,1,0:T(8,128)(2,1)S(1)}, u32[]{:S(2)}, u32[]{:S(2)}) %all-to-all-start.1) | async-done | bytes 786464 | tf_op jit(solution)/shard_map/all_to_all | solution.py:122
  187.1 1.4 bitcast_convert_fusion
  188.5 5.1 %gather_fusion = f32[512,1024]{1,0:T(8,128)} fusion(f32[384,1024]{1,0:T(8,128)} %bitcast_convert_fusion, s32[1024]{0:T(1024)S(1)} %pad_clamp_fusion), kind=kCustom, calls=%fused_computation | custom fusion | bytes 4196352 | tf_op jit(solution)/shard_map/jit(_take)/gather | solution.py:47
  193.5 3.0 %fusion.15 = bf16[64,1024]{1,0:T(8,128)(2,1)} fusion(f32[512,1024]{1,0:T(8,128)} %gather_fusion, f32[64,8]{1,0:T(8,128)S(1)} %copy.71, pred[64,8]{1,0:T(8,128)(4,1)S(1)} %copy.63), kind=kLoop, calls=%fused_computation.14 | loop fusion | flops 1507328 | bytes 2230784 | tf_op jit(solution)/shard_map/reduce_sum | solution.py:51
  196.6 0.0 reduce-scatter.5.cloned.1.call-update
  196.6 5.9 %reduce-scatter.5.cloned.1.call-done = bf16[64,512]{1,0:T(8,128)(2,1)} async-done(((bf16[64,1024]{1,0:T(8,128)(2,1)}), bf16[64,512]{1,0:T(8,128)(2,1)}) %reduce-scatter.5.cloned.1.call-update) | async-done | bytes 65552 | tf_op jit(solution)/shard_map/reduce_scatter | solution.py:130
  202.5 1.5 add_convert_fusion
  (27 shorter events, 0.2 us)
Async XLA Ops:
  6.5 12.4 %copy-start = (bf16[1024,1024]{1,0:T(8,128)(2,1)S(1)}, bf16[1024,1024]{1,0:T(8,128)(2,1)}, u32[]{:S(2)}) copy-start(bf16[1024,1024]{1,0:T(8,128)(2,1)} %param.20) | copy-start | bytes 6291460
  6.5 33.5 %all-reduce.2.cloned.1.call-start = ((), (), s32[]{:S(2)}) async-start(), calls=%async_computation.4 | async-start | bytes 262144 | tf_op jit(solution)/shard_map/psum | solution.py:76
  10.6 9.5 %copy-start.3 = (s32[64,8]{0,1:T(8,128)S(1)}, s32[64,8]{0,1:T(8,128)}, u32[]{:S(2)}) copy-start(s32[64,8]{0,1:T(8,128)} %param.23) | copy-start | bytes 6148
  12.9 27.1 %copy-start.2 = (bf16[64,1024]{1,0:T(8,128)(2,1)S(1)}, bf16[64,1024]{1,0:T(8,128)(2,1)}, u32[]{:S(2)}) copy-start(bf16[64,1024]{1,0:T(8,128)(2,1)} %param.21) | copy-start | bytes 393220
  13.0 33.0 %copy-start.5 = (f32[1024]{0:T(1024)S(1)}, f32[1024]{0:T(1024)}, u32[]{:S(2)}) copy-start(f32[1024]{0:T(1024)} %param.22) | copy-start | bytes 12292
  20.1 139.5 %reduce-scatter.3.cloned.1.call-start = ((), (), s32[]{:S(2)}) async-start(), calls=%async_computation.5 | async-start | bytes 3145728 | tf_op jit(solution)/shard_map/reduce_scatter | solution.py:119
  100.2 1.1 copy-start.1
  128.5 38.8 %copy-start.4 = (f32[64,8]{0,1:T(8,128)S(1)}, f32[64,8]{0,1:T(8,128)}, u32[]{:S(2)}) copy-start(f32[64,8]{0,1:T(8,128)} %param.24) | copy-start | bytes 6148
  162.5 24.5 %all-to-all-start.1 = ((bf16[4,96,1024]{2,1,0:T(8,128)(2,1)}), bf16[4,96,1024]{2,1,0:T(8,128)(2,1)S(1)}, u32[]{:S(2)}, u32[]{:S(2)}) async-start(bf16[4,96,1024]{2,1,0:T(8,128)(2,1)} %copy.69), calls=%async_computation.2 | async-start | bytes 1572864 | tf_op jit(solution)/shard_map/all_to_all | solution.py:122
  167.1 35.3 %reduce-scatter.5.cloned.1.call-start = ((), (), s32[]{:S(2)}) async-start(), calls=%async_computation.6 | async-start | bytes 196608 | tf_op jit(solution)/shard_map/reduce_scatter | solution.py:130
Sparse Core Ops, SparseCore 0:
  20.2 19.6 all-reduce.1
  128.6 30.9 reduce-scatter.2
  196.7 5.7 reduce-scatter.4
where the time goes:
time: 211 us; the launch traced here: 210 us
  waiting for transfers between devices  73.9 us (35%)
  blocking collectives  56.3 us (27%)
  matrix products  33.7 us (16%)
  local copies, waits for them, and re-layouts  17.4 us (8%)
  between operations  13.3 us (6%)
  other arithmetic  11.3 us (5%)
  starting transfers between devices  4.62 us (2%)
    all_to_all x1, blocking collectives, on_device(): lax.all_to_all(outgoing.reshape(ep_count, local_experts, capacity, width)...  39.8 us
    reduce_scatter x1, waiting for transfers between devices, on_device(): lax.psum_scatter(expert_out.astype(jnp.float32).astype(jnp.bfloat16), 'ha...  31.1 us
    all_to_all x1, waiting for transfers between devices, on_device(): lax.all_to_all(summed.reshape(ep_count, local_experts * capacity, half_wi...  19.5 us
    dot_general x1, matrix products, on_device(): jnp.einsum('secf,efd->secd', activation, w_down, preferred_element_type=j...  18.4 us
    psum x1, waiting for transfers between devices, on_device(): mixed = lax.psum(partial_mix.astype(jnp.bfloat16), 'tp').astype(jnp.float32)  17.3 us
    dot_general x1, matrix products, on_device(): jnp.einsum('secd,efd->secf', arrived, w_gate, preferred_element_type=jnp....  8.68 us
    reshape x2, local copies, waits for them, and re-layouts, on_device(): outgoing.reshape(ep_count, local_experts, capacity, width)  6.06 us
    all_gather x1, blocking collectives, on_device(): lax.all_gather(attended, 'half', axis=0, tiled=True)  6 us
  transfers between devices with their start and end apart: 4, of which 4 were waited for; matrix products, arithmetic and copies ran while one was open for 1% of the time, Pallas kernels for 0%

commit v1 on v0

--- a/solution.py
+++ b/solution.py
@@ -6,6 +6,22 @@
 
 EXPERTS = 64
 EPSILON = 1e-06
+
+
+def exchange_in_pairs(x, axis, split, join):
+    ways, here = (lax.axis_size(axis), lax.axis_index(axis))
+    width = x.shape[split] // ways
+    lengths = list(x.shape)
+    lengths[split] = width
+    height = lengths[join]
+    lengths[join] = height * ways
+    full = jnp.zeros(lengths, x.dtype)
+    for mask in range(ways):
+        part = lax.dynamic_slice_in_dim(x, (here ^ mask) * width, width, axis=split)
+        if mask:
+            part = lax.ppermute(part, axis, [(d, d ^ mask) for d in range(ways)])
+        full = lax.dynamic_update_slice_in_dim(full, part, (here ^ mask) * height, axis=join)
+    return full
 
 
 def attend(queries, new_keys, new_values, cache_keys, cache_values, lengths):
@@ -119,12 +135,11 @@
     summed = lax.psum_scatter(
         expert_out.astype(jnp.float32).astype(jnp.bfloat16), "half", scatter_dimension=3, tiled=True
     ).astype(jnp.float32)
-    returned = lax.all_to_all(
+    returned = exchange_in_pairs(
         summed.reshape(ep_count, local_experts * capacity, half_width).astype(jnp.bfloat16),
         "ep",
-        split_axis=0,
-        concat_axis=0,
-        tiled=True,
+        0,
+        0,
     ).astype(jnp.float32)
     term = combine_rows(returned.reshape(slot_count, half_width), target, gates)
     expert_sum = lax.psum_scatter(

time: 211 us -> 225 us (1.066)
  waiting for transfers between devices: 73.9 us -> 86.8 us
    ppermute x0 -> x3, waiting for transfers between devices: none -> 26.6 us  [exchange_in_pairs(): part = lax.ppermute(part, axis, [(d, d ^ mask) for d in range(ways)])]
    all_to_all x1 -> x0, waiting for transfers between devices: 19.5 us -> none  [on_device(): lax.all_to_all(summed.reshape(ep_count, local_experts * capacity, half_wi...]
    reduce_scatter x1, waiting for transfers between devices: 5.87 us -> 12.7 us  [on_device(): lax.psum_scatter(term.astype(jnp.bfloat16), 'tp', scatter_dimension=1, ti...]
    all_to_all x1 -> x0, starting transfers between devices: 4.58 us -> none  [on_device(): lax.all_to_all(summed.reshape(ep_count, local_experts * capacity, half_wi...]
    ppermute x0 -> x3, starting transfers between devices: none -> 4.45 us  [exchange_in_pairs(): part = lax.ppermute(part, axis, [(d, d ^ mask) for d in range(ways)])]
  transfers between devices with their start and end apart: 4 -> 6, of which waited for: 4 -> 5; matrix products, arithmetic and copies ran while one was open for 1% -> 1% of each run, Pallas kernels for 0% -> 0%
where the time goes in v1:
time: 225 us
  waiting for transfers between devices  86.8 us (39%)
  blocking collectives  56.3 us (25%)
  matrix products  33.7 us (15%)
  local copies, waits for them, and re-layouts  18.4 us (8%)
  between operations  13.4 us (6%)
  other arithmetic  11.3 us (5%)
  starting transfers between devices  4.76 us (2%)
    all_to_all x1, blocking collectives, on_device(): lax.all_to_all(outgoing.reshape(ep_count, local_experts, capacity, width)...  39.8 us
    reduce_scatter x1, waiting for transfers between devices, on_device(): lax.psum_scatter(expert_out.astype(jnp.float32).astype(jnp.bfloat16), 'ha...  30.2 us
    ppermute x3, waiting for transfers between devices, exchange_in_pairs(): part = lax.ppermute(part, axis, [(d, d ^ mask) for d in range(ways)])  26.6 us
    dot_general x1, matrix products, on_device(): jnp.einsum('secf,efd->secd', activation, w_down, preferred_element_type=j...  18.4 us
    psum x1, waiting for transfers between devices, on_device(): mixed = lax.psum(partial_mix.astype(jnp.bfloat16), 'tp').astype(jnp.float32)  17.3 us
    reduce_scatter x1, waiting for transfers between devices, on_device(): lax.psum_scatter(term.astype(jnp.bfloat16), 'tp', scatter_dimension=1, ti...  12.7 us
    dot_general x1, matrix products, on_device(): jnp.einsum('secd,efd->secf', arrived, w_gate, preferred_element_type=jnp....  8.69 us
    reshape x2, local copies, waits for them, and re-layouts, on_device(): outgoing.reshape(ep_count, local_experts, capacity, width)  6.06 us
  transfers between devices with their start and end apart: 6, of which 5 were waited for; matrix products, arithmetic and copies ran while one was open for 1% of the time, Pallas kernels for 0%

profile of v1, /device:TPU:0, one launch (start us, length us, event | category | flops | bytes accessed | tf_op | source)
XLA Modules:
  0.0 224.7 jit_solution(9612071119026510143)
XLA Ops:
  6.5 1.0 copy.90
  7.5 0.7 iota_compare_fusion.3
  8.3 0.8 fusion.58
  9.1 1.5 fusion.76
  10.6 0.2 fusion.55
  10.9 0.7 convert_element_type.73
  11.6 1.4 fusion.41
  13.0 6.0 %all_gather.6 = bf16[64,1024]{1,0:T(8,128)(2,1)S(1)} all-gather(bf16[32,1024]{1,0:T(8,128)(2,1)S(1)} %bitcast.97), channel_id=1, replica_groups=mesh['groups'=2,'ep'=4,'half'=2,'tp'=2] {'half'}, dimensions={0}, use_global_device_ids=true | all-gather | bytes 196608 | tf_op jit(solution)/shard_map/all_gather | solution.py:88
  19.0 1.1 convolution_convert_fusion.1
  20.2 0.1 copy.68
  20.3 0.1 eq.56
  20.4 0.1 eq.52
  20.5 1.2 reduce-window.6
  21.7 0.2 slice_reduce_fusion
  22.0 0.1 fusion.53
  22.1 0.1 reduce_sum.49
  22.3 0.1 copy.73
  22.4 0.3 fusion.47
  22.7 17.3 %all-reduce.2.cloned.1.call-done = bf16[64,1024]{1,0:T(8,128)(2,1)} async-done(((bf16[64,1024]{1,0:T(8,128)(2,1)}), bf16[64,1024]{1,0:T(8,128)(2,1)}) %all-reduce.2.cloned.1.call-update) | async-done | bytes 131088 | tf_op jit(solution)/shard_map/psum | solution.py:92
  40.0 1.0 convert_add_fusion
  41.0 4.9 %psum.15 = f32[64]{0:T(128)S(1)} all-reduce(f32[64]{0:T(128)S(1)} %get-tuple-element.12), channel_id=1, replica_groups=mesh['groups'=2,'ep'=4,'half'=2,'tp'=2] {'half'}, use_global_device_ids=true, to_apply=%region_8.9 | all-reduce | flops 64 | bytes 512 | tf_op jit(solution)/shard_map/psum | solution.py:94
  46.0 1.0 multiply_convert_fusion
  47.0 5.6 %all_gather.7 = bf16[64,2048]{1,0:T(8,128)(2,1)S(1)} all-gather(bf16[64,1024]{1,0:T(8,128)(2,1)S(1)} %multiply_convert_fusion), channel_id=1, replica_groups=mesh['groups'=2,'ep'=4,'half'=2,'tp'=2] {'half'}, dimensions={1}, use_global_device_ids=true | all-gather | bytes 393216 | tf_op jit(solution)/shard_map/all_gather | solution.py:118
  52.6 1.8 convolution_convert_fusion
  54.4 3.6 %reshape.224 = bf16[4,8,12,2048]{3,2,1,0:T(8,128)(2,1)} reshape(bf16[384,2048]{1,0:T(8,128)(2,1)} %convolution_convert_fusion) | data formatting | bytes 3145728 | tf_op jit(solution)/shard_map/reshape | solution.py:123
  58.0 2.5 %copy.74 = bf16[4,8,12,2048]{3,1,2,0:T(8,128)(2,1)S(1)} copy(bf16[4,8,12,2048]{3,2,1,0:T(8,128)(2,1)} %reshape.224) | data formatting | bytes 3145728 | tf_op jit(solution)/shard_map/reshape | solution.py:123
  60.5 39.8 %all_to_all.5 = bf16[4,8,12,2048]{3,1,2,0:T(8,128)(2,1)S(1)} all-to-all(bf16[4,8,12,2048]{3,1,2,0:T(8,128)(2,1)S(1)} %copy.74), channel_id=1, replica_groups=mesh['groups'=2,'ep'=4,'half'=2,'tp'=2] {'ep'}, dimensions={0} | all-to-all | bytes 3145728 | tf_op jit(solution)/shard_map/all_to_all | solution.py:122
  100.2 1.1 copy-done.1
  101.4 8.7 %fusion.16 = f32[4,8,12,384]{3,2,0,1:T(8,128)S(1)} fusion(bf16[8,384,2048]{2,1,0:T(8,128)(2,1)} %param.25, bf16[4,8,12,2048]{3,1,2,0:T(8,128)(2,1)S(1)} %all_to_all.5), kind=kOutput, calls=%fused_computation.15 | convolution fusion | flops 603979776 | bytes 14745600 | tf_op jit(solution)/shard_map/secd,efd->secf/dot_general | solution.py:129
  110.1 18.4 %fusion.9 = bf16[4,8,12,2048]{3,2,0,1:T(8,128)(2,1)} fusion(bf16[8,384,2048]{2,1,0:T(8,128)(2,1)} %param.27, bf16[8,384,2048]{2,1,0:T(8,128)(2,1)} %param.26, bf16[4,8,12,2048]{3,1,2,0:T(8,128)(2,1)} %copy-done.1, f32[4,8,12,384]{3,2,0,1:T(8,128)S(1)} %fusion.16), kind=kOutput, calls=%fused_computation.9 | convolution fusion | flops 1209630720 | bytes 28901376 | tf_op jit(solution)/shard_map/secf,efd->secd/dot_general | solution.py:132
  128.5 0.3 reduce-scatter.5.cloned.1.call-start
  128.9 0.1 reshape.227
  129.0 0.2 copy-done.4
  129.2 0.1 copy.83
  129.3 0.1 copy.72
  129.4 30.2 %reduce-scatter.3.cloned.1.call-done = bf16[4,8,12,1024]{3,2,0,1:T(8,128)(2,1)} async-done(((bf16[4,8,12,2048]{3,2,0,1:T(8,128)(2,1)}), bf16[4,8,12,1024]{3,2,0,1:T(8,128)(2,1)}) %reduce-scatter.3.cloned.1.call-update) | async-done | bytes 786448 | tf_op jit(solution)/shard_map/reduce_scatter | solution.py:135
  159.6 1.8 copy.77
  161.4 1.6 constant_dynamic-slice_fusion
  163.1 1.5 collective-permute-start
  164.6 2.4 %collective-permute-start.1 = (bf16[1,96,1024]{2,0,1:T(2,128)(2,1)S(1)}, bf16[1,96,1024]{2,0,1:T(2,128)(2,1)S(1)}, u32[]{:S(2)}, u32[]{:S(2)}) collective-permute-start(bf16[1,96,1024]{2,0,1:T(2,128)(2,1)S(1)} %get-tuple-element.8), channel_id=1, source_target_pairs={{0,8},{4,12},{8,0},{12,4},{1,9},{5,13},{9,1},{13,5},{2,10},{6,14},... | collective-permute-start | bytes 589832 | tf_op jit(solution)/shard_map/ppermute | solution.py:22
  167.0 0.5 collective-permute-start.2
  167.7 13.7 %collective-permute-done = bf16[1,96,1024]{2,0,1:T(2,128)(2,1)S(1)} collective-permute-done((bf16[1,96,1024]{2,0,1:T(2,128)(2,1)S(1)}, bf16[1,96,1024]{2,0,1:T(2,128)(2,1)S(1)}, u32[]{:S(2)}, u32[]{:S(2)}) %collective-permute-start) | collective-permute-done | bytes 196640 | tf_op jit(solution)/shard_map/ppermute | solution.py:22
  181.4 12.9 %collective-permute-done.1 = bf16[1,96,1024]{2,0,1:T(2,128)(2,1)S(1)} collective-permute-done((bf16[1,96,1024]{2,0,1:T(2,128)(2,1)S(1)}, bf16[1,96,1024]{2,0,1:T(2,128)(2,1)S(1)}, u32[]{:S(2)}, u32[]{:S(2)}) %collective-permute-start.1) | collective-permute-done | bytes 196640 | tf_op jit(solution)/shard_map/ppermute | solution.py:22
  194.5 1.4 bitcast_convert_fusion
  195.9 5.1 %gather_fusion = f32[512,1024]{1,0:T(8,128)} fusion(f32[384,1024]{1,0:T(8,128)} %bitcast_convert_fusion, s32[1024]{0:T(1024)S(1)} %pad_clamp_fusion), kind=kCustom, calls=%fused_computation | custom fusion | bytes 4196352 | tf_op jit(solution)/shard_map/jit(_take)/gather | solution.py:63
  201.0 3.0 %fusion.15 = bf16[64,1024]{1,0:T(8,128)(2,1)} fusion(f32[512,1024]{1,0:T(8,128)} %gather_fusion, f32[64,8]{1,0:T(8,128)S(1)} %copy.83, pred[64,8]{1,0:T(8,128)(4,1)S(1)} %copy.72), kind=kLoop, calls=%fused_computation.14 | loop fusion | flops 1507328 | bytes 2230784 | tf_op jit(solution)/shard_map/reduce_sum | solution.py:67
  204.0 12.7 %reduce-scatter.5.cloned.1.call-done = bf16[64,512]{1,0:T(8,128)(2,1)} async-done(((bf16[64,1024]{1,0:T(8,128)(2,1)}), bf16[64,512]{1,0:T(8,128)(2,1)}) %reduce-scatter.5.cloned.1.call-update) | async-done | bytes 65552 | tf_op jit(solution)/shard_map/reduce_scatter | solution.py:145
  216.7 1.5 add_convert_fusion
  (36 shorter events, 0.8 us)
Async XLA Ops:
  6.5 12.4 %copy-start = (bf16[1024,1024]{1,0:T(8,128)(2,1)S(1)}, bf16[1024,1024]{1,0:T(8,128)(2,1)}, u32[]{:S(2)}) copy-start(bf16[1024,1024]{1,0:T(8,128)(2,1)} %param.20) | copy-start | bytes 6291460
  6.5 33.5 %all-reduce.2.cloned.1.call-start = ((), (), s32[]{:S(2)}) async-start(), calls=%async_computation.3 | async-start | bytes 262144 | tf_op jit(solution)/shard_map/psum | solution.py:92
  10.6 9.5 %copy-start.3 = (s32[64,8]{0,1:T(8,128)S(1)}, s32[64,8]{0,1:T(8,128)}, u32[]{:S(2)}) copy-start(s32[64,8]{0,1:T(8,128)} %param.23) | copy-start | bytes 6148
  12.9 27.1 %copy-start.2 = (bf16[64,1024]{1,0:T(8,128)(2,1)S(1)}, bf16[64,1024]{1,0:T(8,128)(2,1)}, u32[]{:S(2)}) copy-start(bf16[64,1024]{1,0:T(8,128)(2,1)} %param.21) | copy-start | bytes 393220
  13.0 33.0 %copy-start.5 = (f32[1024]{0:T(1024)S(1)}, f32[1024]{0:T(1024)}, u32[]{:S(2)}) copy-start(f32[1024]{0:T(1024)} %param.22) | copy-start | bytes 12292
  20.1 139.5 %reduce-scatter.3.cloned.1.call-start = ((), (), s32[]{:S(2)}) async-start(), calls=%async_computation.4 | async-start | bytes 3145728 | tf_op jit(solution)/shard_map/reduce_scatter | solution.py:135
  100.2 1.1 copy-start.1
  128.5 0.7 copy-start.4
  128.5 88.2 %reduce-scatter.5.cloned.1.call-start = ((), (), s32[]{:S(2)}) async-start(), calls=%async_computation.5 | async-start | bytes 196608 | tf_op jit(solution)/shard_map/reduce_scatter | solution.py:145
  163.1 18.3 %collective-permute-start = (bf16[1,96,1024]{2,0,1:T(2,128)(2,1)S(1)}, bf16[1,96,1024]{2,0,1:T(2,128)(2,1)S(1)}, u32[]{:S(2)}, u32[]{:S(2)}) collective-permute-start(bf16[1,96,1024]{2,0,1:T(2,128)(2,1)S(1)} %get-tuple-element.9), channel_id=1, source_target_pairs={{0,4},{4,0},{8,12},{12,8},{1,5},{5,1},{9,13},{13,9},{2,6},{6,2},{1... | collective-permute-start | bytes 589832 | tf_op jit(solution)/shard_map/ppermute | solution.py:22
  164.6 29.7 %collective-permute-start.1 = (bf16[1,96,1024]{2,0,1:T(2,128)(2,1)S(1)}, bf16[1,96,1024]{2,0,1:T(2,128)(2,1)S(1)}, u32[]{:S(2)}, u32[]{:S(2)}) collective-permute-start(bf16[1,96,1024]{2,0,1:T(2,128)(2,1)S(1)} %get-tuple-element.8), channel_id=1, source_target_pairs={{0,8},{4,12},{8,0},{12,4},{1,9},{5,13},{9,1},{13,5},{2,10},{6,14},... | collective-permute-start | bytes 589832 | tf_op jit(solution)/shard_map/ppermute | solution.py:22
  167.0 27.4 %collective-permute-start.2 = (bf16[1,96,1024]{2,0,1:T(2,128)(2,1)S(1)}, bf16[1,96,1024]{2,0,1:T(2,128)(2,1)S(1)}, u32[]{:S(2)}, u32[]{:S(2)}) collective-permute-start(bf16[1,96,1024]{2,0,1:T(2,128)(2,1)S(1)} %get-tuple-element.7), channel_id=1, source_target_pairs={{0,12},{4,8},{8,4},{12,0},{1,13},{5,9},{9,5},{13,1},{2,14},{6,10},... | collective-permute-start | bytes 589832 | tf_op jit(solution)/shard_map/ppermute | solution.py:22
Sparse Core Ops, SparseCore 0:
  20.2 19.6 all-reduce.1
  128.6 30.9 reduce-scatter.2
  204.1 12.5 reduce-scatter.4
